TPU v7x, 32 devices: a whole 2x2x4 slice. The times are simulated.
32 devices in a mesh: groups: 2 (over x), lon: 16 (over z, y, core).
Axes of the slice: x: 2, y: 2, z: 4, core: 2. Of those that a mesh axis runs over, the one named last changes fastest.
Arguments:
- fields: bfloat16 [128, 512, 256], P('groups', 'lon'), parts along dimension 0, may hold values from -36 to 36
- sea_mask: int32 [128, 512], P('groups', 'lon'), parts along dimension 0, may hold values 0 or 1
- cotangent: bfloat16 [128, 512, 256], P('groups', 'lon'), parts along dimension 0, may hold values from -6 to 6
- depth_kernel: float32 [7, 7, 256], replicated, may hold values from -0.875 to 0.875
- norm_gain: float32 [256], replicated, may hold values from 0.1 to 1.9
- up_weight: bfloat16 [256, 1024], replicated, may hold values from -0.375 to 0.375
- down_weight: bfloat16 [256, 1024], replicated, may hold values from -0.1875 to 0.1875
- layer_scale: float32 [256], replicated, may hold values from 0.3 to 3
Outputs:
- grad_fields: bfloat16 [128, 512, 256], P('groups', 'lon'), parts along dimension 0
- grad_kernel: float32 [14, 7, 256], P('groups'), parts along dimension 0
- grad_up: float32 [256, 2048], P('lon', 'groups'), parts along dimension 1
- grad_down: float32 [256, 2048], P('lon', 'groups'), parts along dimension 1
There are 2 independent parts, one for each index of `groups`. A program takes and returns all parts, laid end to end along the dimension named above; an argument that names none is the same for every part. Nothing has to cross between parts.
All inputs are finite; a program needn't handle non-finite values. No bound on the sum of `sea_mask` on one device may be relied on, other than what follows from the above.
Results may differ from a plain program's by a relative error of at most 0.0063.
Values may be sent and summed in bfloat16 or wider, within the bound.
A program may use at most 128 MiB of HBM per device.

v0:
```python
import math
import jax
import jax.numpy as jnp
from jax import lax
from jax.sharding import PartitionSpec as P


def from_partner(block, axis, bit):
    count = lax.axis_size(axis)
    route = []
    for low in range(count):
        high = low | 1 << bit
        if high != low and high < count:
            route += [(low, high), (high, low)]
    return lax.ppermute(block, axis, route)


def extended_2(cells, sides, width):
    for axis, dim in sides:
        count = lax.axis_size(axis)
        head = lax.slice_in_dim(cells, 0, width, axis=dim)
        tail = lax.slice_in_dim(cells, cells.shape[dim] - width, cells.shape[dim], axis=dim)
        cells = jnp.concatenate(
            [
                lax.ppermute(tail, axis, [(i, (i + 1) % count) for i in range(count)]),
                cells,
                lax.ppermute(head, axis, [((i + 1) % count, i) for i in range(count)]),
            ],
            axis=dim,
        )
    return cells


def gelu_tanh(values):
    return jax.nn.gelu(values, approximate=True)


def local(
    fields, sea_mask, cotangent, depth_kernel, norm_gain, up_weight, down_weight, layer_scale
):
    band_rows, band_cols, channels = fields.shape
    devices = lax.axis_size("lon")
    mask_bf = sea_mask.astype(jnp.bfloat16)[:, :, None]
    masked = fields * mask_bf
    seam_rows = masked[band_rows - 3 :]
    partner_rows = seam_rows
    for bit in range(devices.bit_length() - 1):
        partner_rows = from_partner(partner_rows, "lon", bit)
    ghost = partner_rows[::-1, ::-1]
    south = jnp.zeros((3, band_cols, channels), jnp.bfloat16)
    padded = jnp.concatenate([south, masked, ghost], axis=0)
    extended = extended_2(padded, (("lon", 1),), 3)
    ext_wide = extended.astype(jnp.float32)
    conv = jnp.zeros((band_rows, band_cols, channels), jnp.float32)
    for row_tap in range(7):
        for col_tap in range(7):
            conv = (
                conv
                + depth_kernel[row_tap, col_tap]
                * ext_wide[row_tap : row_tap + band_rows, col_tap : col_tap + band_cols]
            )
    mean_z = jnp.mean(conv, axis=-1, keepdims=True)
    centred = conv - mean_z
    inv_std = lax.rsqrt(jnp.mean(centred * centred, axis=-1, keepdims=True) + 1e-06)
    nhat = centred * inv_std
    cells = band_rows * band_cols
    normed = (nhat * norm_gain).astype(jnp.bfloat16).reshape(cells, channels)
    dout = (
        (cotangent.astype(jnp.float32) * layer_scale * mask_bf.astype(jnp.float32))
        .astype(jnp.bfloat16)
        .reshape(cells, channels)
    )
    preact = jnp.dot(normed, up_weight, preferred_element_type=jnp.float32)
    hidden = gelu_tanh(preact).astype(jnp.bfloat16)
    dhid = jnp.dot(dout, down_weight, preferred_element_type=jnp.float32)
    _, back = jax.vjp(gelu_tanh, preact)
    dpre = back(dhid)[0].astype(jnp.bfloat16)
    contract_rows = (((0,), (0,)), ((), ()))
    contract_cols = (((1,), (1,)), ((), ()))
    factor = 1.0 / math.sqrt(cells * devices)
    hidden_width = up_weight.shape[1]
    term_up = lax.dot_general(normed, dpre, contract_rows, preferred_element_type=jnp.float32)
    term_down = lax.dot_general(dout, hidden, contract_rows, preferred_element_type=jnp.float32)
    owned = lax.psum_scatter(
        jnp.concatenate([term_up, term_down], axis=1) * factor,
        "lon",
        scatter_dimension=0,
        tiled=True,
    )
    grad_up = owned[:, :hidden_width]
    grad_down = owned[:, hidden_width:]
    dnorm = lax.dot_general(dpre, up_weight, contract_cols, preferred_element_type=jnp.float32)
    scaled = dnorm.reshape(band_rows, band_cols, channels) * norm_gain
    grad_conv = inv_std * (
        scaled
        - jnp.mean(scaled, axis=-1, keepdims=True)
        - nhat * jnp.mean(scaled * nhat, axis=-1, keepdims=True)
    )
    taps = []
    for row_tap in range(7):
        for col_tap in range(7):
            taps.append(
                jnp.sum(
                    grad_conv
                    * ext_wide[row_tap : row_tap + band_rows, col_tap : col_tap + band_cols],
                    axis=(0, 1),
                )
            )
    local_kernel = jnp.stack(taps, axis=0).reshape(7, 7, channels) * factor
    grad_kernel = lax.psum(local_kernel, "lon")
    grad_pad = jnp.pad(grad_conv, ((6, 6), (6, 6), (0, 0)))
    grad_ext = jnp.zeros((band_rows + 6, band_cols + 6, channels), jnp.float32)
    for row_tap in range(7):
        for col_tap in range(7):
            grad_ext = (
                grad_ext
                + depth_kernel[row_tap, col_tap]
                * grad_pad[
                    6 - row_tap : 12 - row_tap + band_rows, 6 - col_tap : 12 - col_tap + band_cols
                ]
            )
    rims = jnp.concatenate([grad_ext[:, :3], grad_ext[:, band_cols + 3 :]], axis=1)
    arrived = extended_2(rims.astype(jnp.bfloat16), (("lon", 1),), 3).astype(rims.dtype)
    grad_padded = grad_ext[:, 3 : band_cols + 3]
    grad_padded = grad_padded.at[:, :3].add(arrived[:, :3])
    grad_padded = grad_padded.at[:, band_cols - 3 :].add(arrived[:, 9:])
    seam_grads = grad_padded[band_rows + 3 :]
    partner_grads = seam_grads
    for bit in range(devices.bit_length() - 1):
        partner_grads = from_partner(partner_grads.astype(jnp.bfloat16), "lon", bit).astype(
            partner_grads.dtype
        )
    grad_masked = grad_padded[3 : band_rows + 3]
    grad_masked = grad_masked.at[band_rows - 3 :].add(partner_grads[::-1, ::-1])
    grad_fields = (
        cotangent.astype(jnp.float32) + mask_bf.astype(jnp.float32) * grad_masked
    ).astype(jnp.bfloat16)
    return (grad_fields, grad_kernel, grad_up, grad_down)


def solution(mesh):
    return jax.shard_map(
        local,
        mesh=mesh,
        in_specs=(
            P("groups", "lon", None),
            P("groups", "lon"),
            P("groups", "lon", None),
            P(),
            P(),
            P(),
            P(),
            P(),
        ),
        out_specs=(
            P("groups", "lon", None),
            P("groups", None, None),
            P("lon", "groups"),
            P("lon", "groups"),
        ),
        check_vma=False,
    )
```

profile of v0, /device:TPU:0, one launch (start us, length us, event | category | flops | bytes accessed | tf_op | source)
XLA Modules:
  0.0 221.3 jit_solution(10699872550884711838)
XLA Ops:
  7.2 0.0 copy-start
  7.2 0.0 copy-start.9
  7.2 0.0 reduce-scatter.2.cloned.1.call-start
  7.2 0.8 convert_element_type.47
  8.1 0.1 copy.15
  8.2 1.6 broadcast_multiply_fusion
  9.8 0.0 copy-start.5
  9.8 0.5 collective-permute-start
  10.3 0.1 copy.14
  10.4 0.8 collective-permute-done
  11.2 2.9 %collective-permute-start.1 = (bf16[3,32,256]{2,1,0:T(8,128)(2,1)S(1)}, bf16[3,32,256]{2,1,0:T(8,128)(2,1)S(1)}, u32[]{:S(2)}, u32[]{:S(2)}) collective-permute-start(bf16[3,32,256]{2,1,0:T(8,128)(2,1)S(1)} %collective-permute-done), channel_id=1, source_target_pairs={{0,2},{2,0},{1,3},{3,1},{4,6},{6,4},{5,7},{7,5},{8,10},{10,8},{9,1... | collective-permute-start | bytes 147464 | tf_op jit(solution)/shard_map/ppermute | solution.py:15
  14.0 1.3 fusion.106
  15.4 0.7 collective-permute-done.1
  16.1 2.1 collective-permute-start.2
  18.3 2.0 collective-permute-done.2
  20.3 3.0 %collective-permute-start.3 = (bf16[3,32,256]{2,1,0:T(8,128)(2,1)S(1)}, bf16[3,32,256]{2,1,0:T(8,128)(2,1)S(1)}, u32[]{:S(2)}, u32[]{:S(2)}) collective-permute-start(bf16[3,32,256]{2,1,0:T(8,128)(2,1)S(1)} %collective-permute-done.2), channel_id=1, source_target_pairs={{0,8},{8,0},{1,9},{9,1},{2,10},{10,2},{3,11},{11,3},{4,12},{12,4},... | collective-permute-start | bytes 147464 | tf_op jit(solution)/shard_map/ppermute | solution.py:15
  23.3 0.6 fusion.119
  24.0 1.4 collective-permute-done.3
  25.4 0.1 rev.6
  25.5 0.1 pad_maximum_fusion.5
  25.6 0.1 collective-permute-start.4
  25.6 4.4 %collective-permute-start.5 = (bf16[70,3,256]{2,1,0:T(4,128)(2,1)S(1)}, bf16[70,3,256]{2,1,0:T(4,128)(2,1)S(1)}, u32[]{:S(2)}, u32[]{:S(2)}) collective-permute-start(bf16[70,3,256]{2,1,0:T(4,128)(2,1)S(1)} %get-tuple-element.97), channel_id=1, source_target_pairs={{1,0},{2,1},{3,2},{4,3},{5,4},{6,5},{7,6},{8,7},{9,8},{10,9},{11,1... | collective-permute-start | bytes 322568 | tf_op jit(solution)/shard_map/ppermute | solution.py:27
  30.2 0.0 copy-start.88
  30.3 2.7 %collective-permute-done.4 = bf16[70,3,256]{2,1,0:T(4,128)(2,1)S(1)} collective-permute-done((bf16[70,3,256]{2,1,0:T(4,128)(2,1)S(1)}, bf16[70,3,256]{2,1,0:T(4,128)(2,1)S(1)}, u32[]{:S(2)}, u32[]{:S(2)}) %collective-permute-start.4) | collective-permute-done | bytes 107552 | tf_op jit(solution)/shard_map/ppermute | solution.py:25
  33.0 1.9 maximum_convert_fusion
  35.2 15.9 %fusion.115 = (f32[64,32]{1,0:T(8,128)S(1)}, f32[64,32,256]{2,1,0:T(8,128)}) fusion(f32[70,38,256]{2,1,0:T(8,128)S(1)} %maximum_convert_fusion, f32[256]{0:T(256)S(1)} %bitcast.211, f32[256]{0:T(256)S(1)} %bitcast.213, f32[256]{0:T(256)S(1)} %bitcast.119, f32[256]{0:T(256)S(1)} %bitcast.121, f32[256]{0:T(256)S(1)} %bitcast.123, f32[256]{0:T(256)S(1)} %bitcast.125, ...), kind=kLoop, calls=%fused_computation.242 | loop fusion | flops 51378176 | bytes 104915968 | tf_op jit(solution)/shard_map/reduce_sum | solution.py:62
  51.1 2.4 %multiply_reduce_fusion.51 = f32[64,32]{1,0:T(8,128)S(1)} fusion(f32[64,32,256]{2,1,0:T(8,128)} %get-tuple-element.93, f32[64,32]{1,0:T(8,128)S(1)} %broadcast_multiply_fusion.3), kind=kLoop, calls=%fused_computation.216 | loop fusion | flops 1570816 | bytes 2113536 | tf_op jit(solution)/shard_map/reduce_sum | solution.py:64
  53.5 0.7 multiply_convert_fusion.2
  54.3 1.3 fusion.121
  55.6 0.3 copy-done.11
  55.9 4.2 %fusion.7 = f32[256,1024]{1,0:T(8,128)} fusion(bf16[2048,256]{1,0:T(8,128)(2,1)S(1)} %bitcast.115, f32[2048,1024]{1,0:T(8,128)S(1)} %fusion.121), kind=kOutput, calls=%fused_computation.59 | convolution fusion | flops 1092616192 | bytes 10485760 | tf_op jit(solution)/shard_map/dot_general | solution.py:83
  60.1 6.3 %fusion.6 = bf16[2048,1024]{1,0:T(8,128)(2,1)S(1)} fusion(f32[2048,1024]{1,0:T(8,128)S(1)} %fusion.121, bf16[2048,256]{1,0:T(8,128)(2,1)S(1)} %bitcast.116, bf16[256,1024]{1,0:T(8,128)(2,1)S(1)} %copy-done.109), kind=kOutput, calls=%fused_computation.57 | convolution fusion | flops 1115684864 | bytes 14155776 | tf_op jit(solution)/shard_map/dot_general | solution.py:75
  66.3 2.6 %multiply_reduce_fusion.50 = (f32[2048]{0:T(1024)S(1)}, f32[2048,256]{1,0:T(8,128)}) fusion(f32[256]{0:T(256)S(1)} %copy-done.17, bf16[2048,1024]{1,0:T(8,128)(2,1)S(1)} %fusion.6, bf16[256,1024]{1,0:T(8,128)(2,1)S(1)} %copy-done), kind=kOutput, calls=%fused_computation.214 | convolution fusion | flops 1074788352 | bytes 6824960 | tf_op jit(solution)/shard_map/dot_general | solution.py:92
  69.0 0.1 div.17
  69.1 2.9 %multiply_reduce_fusion.49 = f32[64,32]{1,0:T(8,128)S(1)} fusion(f32[64,32,256]{2,1,0:T(8,128)} %bitcast.112, f32[64,32,256]{2,1,0:T(8,128)} %get-tuple-element.93, f32[256]{0:T(256)S(1)} %copy-done.17, f32[64,32]{1,0:T(8,128)S(1)} %add_rsqrt_fusion, f32[64,32]{1,0:T(8,128)S(1)} %broadcast_multiply_fusion.3), kind=kLoop, calls=%fused_computation.213 | loop fusion | flops 2619392 | bytes 4219904 | tf_op jit(solution)/shard_map/reduce_sum | solution.py:97
  72.0 0.5 copy-done.6
  72.9 6.6 %multiply_reduce_fusion = (f32[256]{0:T(256)}, f32[256]{0:T(256)}, f32[256]{0:T(256)}, f32[256]{0:T(256)}, f32[256]{0:T(256)}, /*index=5*/f32[256]{0:T(256)}, f3...) fusion(f32[70,38,256]{2,1,0:T(8,128)S(1)} %maximum_convert_fusi, ...), kind=kLoop, calls=%fused_computation.163 | loop fusion | flops 22539776 | bytes 44092416 | tf_op jit(solution)/shard_map/reduce_sum | solution.py:103
  79.9 22.2 %fusion.113 = (bf16[70,38,256]{2,1,0:T(8,128)(2,1)S(1)}, f32[70,38,256]{2,1,0:T(8,128)S(1)}) fusion(f32[256]{0:T(256)S(1)} %bitcast.212, f32[256]{0:T(256)S(1)} %bitcast.214, f32[256]{0:T(256)S(1)} %bitcast.120, f32[256]{0:T(256)S(1)} %bitcast.122, f32[256]{0:T(256)S(1)} %bitcast.124, f32[256]{0:T(256)S(1)} %bitcast.126, f32[256]{0:T(256)S(1)} %bitcast.128, ...), kind=kLoop, calls=%fused_computation.241 | loop fusion | flops 66734080 | bytes 6233088 | tf_op jit(solution)/shard_map/convert.3
  102.1 0.1 fusion.116
  102.3 0.7 collective-permute-start.6
  103.0 3.8 %collective-permute-start.7 = (bf16[70,3,256]{2,1,0:T(4,128)(2,1)S(1)}, bf16[70,3,256]{2,1,0:T(4,128)(2,1)S(1)}, u32[]{:S(2)}, u32[]{:S(2)}) collective-permute-start(bf16[70,3,256]{2,1,0:T(4,128)(2,1)S(1)} %get-tuple-element.95), channel_id=1, source_target_pairs={{1,0},{2,1},{3,2},{4,3},{5,4},{6,5},{7,6},{8,7},{9,8},{10,9},{11,1... | collective-permute-start | bytes 322568 | tf_op jit(solution)/shard_map/ppermute | solution.py:27
  106.8 4.5 %fusion.122 = f32[256,1024]{1,0:T(8,128)} fusion(bf16[2048,256]{1,0:T(8,128)(2,1)S(1)} %bitcast.114, bf16[2048,1024]{1,0:T(8,128)(2,1)} %copy-done.110), kind=kOutput, calls=%fused_computation.249 | convolution fusion | flops 1073741824 | bytes 6291456 | tf_op jit(solution)/shard_map/dot_general | solution.py:82
  111.3 1.8 slice.866
  113.1 0.6 copy-done.12
  113.7 0.6 copy-done.13
  114.4 1.0 convert_add_fusion.1
  115.4 5.2 %scatter-add.10 = f32[70,32,256]{2,1,0:T(8,128)} dynamic-update-slice(f32[70,32,256]{2,1,0:T(8,128)} %slice.866, f32[70,3,256]{2,1,0:T(4,128)} %convert_add_fusion.1, s32[]{:T(128)} %constant.108.clone.1, s32[]{:T(128)} %constant.108.clone.1, s32[]{:T(128)} %constant.108.clone.1) | dynamic-update-slice | bytes 430084 | tf_op jit(solution)/shard_map/scatter-add | solution.py:125
  120.6 2.1 slice_add_fusion
  122.8 4.6 %scatter-add.11 = f32[70,32,256]{2,1,0:T(8,128)} dynamic-update-slice(f32[70,32,256]{2,1,0:T(8,128)} %scatter-add.10, f32[70,3,256]{2,1,0:T(4,128)} %slice_add_fusion, s32[]{:T(128)} %constant.108.clone.1, s32[]{:T(128)} %constant.109.clone.1, s32[]{:T(128)} %constant.108.clone.1) | dynamic-update-slice | bytes 430084 | tf_op jit(solution)/shard_map/scatter-add | solution.py:126
  127.3 0.9 slice.1409
  128.2 3.2 %maximum_multiply_fusion = f32[256,2048]{1,0:T(8,128)} fusion(f32[256,1024]{1,0:T(8,128)} %fusion.7, f32[256,1024]{1,0:T(8,128)} %fusion.122), kind=kLoop, calls=%fused_computation.162 | loop fusion | flops 1048576 | bytes 4194304 | tf_op jit(solution)/shard_map/mul | solution.py:85
  131.4 0.0 reduce-scatter.2.cloned.1.call-update
  131.5 0.1 collective-permute-start.9
  131.5 6.1 %multiply_reduce_fusion.18 = (f32[256]{0:T(256)S(1)}, f32[256]{0:T(256)S(1)}, f32[256]{0:T(256)S(1)}, f32[256]{0:T(256)S(1)}, f32[256]{0:T(256)S(1)}, /*index=5*...) fusion(f32[64,32,256]{2,1,0:T(8,128)} %copy-done.3, ...), kind=kLoop, calls=%fused_computation.181 | loop fusion | flops 18869760 | bytes 39864320 | tf_op jit(solution)/shard_map/reduce_sum | solution.py:103
  137.9 0.1 collective-permute-start.10
  138.0 4.3 %multiply_reduce_fusion.36 = (f32[256]{0:T(256)S(1)}, f32[256]{0:T(256)S(1)}, f32[256]{0:T(256)S(1)}, f32[256]{0:T(256)S(1)}, f32[256]{0:T(256)}, /*index=5*/f32...) fusion(f32[64,32,256]{2,1,0:T(8,128)S(1)} %copy-done.4, ...), kind=kLoop, calls=%fused_computation.199 | loop fusion | flops 13628160 | bytes 29373440 | tf_op jit(solution)/shard_map/reduce_sum | solution.py:103
  142.4 1.6 stack.199
  144.0 1.8 collective-permute-start.11
  145.8 61.8 %psum.7 = f32[7,7,256]{2,1,0:T(8,128)} all-reduce(f32[7,7,256]{2,1,0:T(8,128)S(1)} %mul.1497), channel_id=1, replica_groups=mesh['groups'=2,'lon'=16] {'lon'}, use_global_device_ids=true, to_apply=%region_53.0 | all-reduce | flops 12544 | bytes 100352 | tf_op jit(solution)/shard_map/psum | solution.py:110
  207.6 1.7 slice.871
  209.4 0.1 rev.7
  209.5 0.9 fusion.108
  210.4 2.5 %fusion.107 = bf16[64,32,256]{2,1,0:T(8,128)(2,1)} fusion(bf16[64,32,256]{2,1,0:T(8,128)(2,1)} %param.16, f32[64,32,256]{2,1,0:T(8,128)S(1)} %fusion.108, f32[64,32]{1,0:T(8,128)S(1)} %copy-done.15), kind=kLoop, calls=%fused_computation.161 | loop fusion | flops 2097152 | bytes 4202496 | tf_op jit(solution)/shard_map/convert_element_type | solution.py:137
  213.0 1.5 fusion.117
  (233 shorter events, 0.5 us)
Async XLA Ops:
  7.2 47.1 %copy-start = (bf16[256,1024]{1,0:T(8,128)(2,1)S(1)}, bf16[256,1024]{1,0:T(8,128)(2,1)}, u32[]{:S(2)}) copy-start(bf16[256,1024]{1,0:T(8,128)(2,1)} %param.19) | copy-start | bytes 1572868
  7.2 205.7 %reduce-scatter.2.cloned.1.call-start = ((), (), s32[]{:S(2)}) async-start(), calls=%async_computation.1 | async-start | bytes 2228224 | tf_op jit(solution)/shard_map/reduce_scatter | solution.py:84
  8.2 10.0 %copy-start.16 = (f32[7,7,256]{2,1,0:T(8,128)S(1)}, f32[7,7,256]{2,1,0:T(8,128)}, u32[]{:S(2)}) copy-start(f32[7,7,256]{2,1,0:T(8,128)} %param.17) | copy-start | bytes 150532
  9.8 23.2 %copy-start.5 = (bf16[64,32,256]{2,1,0:T(8,128)(2,1)}, bf16[64,32,256]{2,1,0:T(8,128)(2,1)S(1)}, u32[]{:S(2)}) copy-start(bf16[64,32,256]{2,1,0:T(8,128)(2,1)S(1)} %broadcast_multiply_fusion) | copy-start | bytes 3145732
  9.8 1.4 collective-permute-start
  10.4 22.6 %copy-start.14 = (f32[64,32]{1,0:T(8,128)}, f32[64,32]{1,0:T(8,128)S(1)}, u32[]{:S(2)}) copy-start(f32[64,32]{1,0:T(8,128)S(1)} %copy.14) | copy-start | bytes 24580
  11.2 4.9 %collective-permute-start.1 = (bf16[3,32,256]{2,1,0:T(8,128)(2,1)S(1)}, bf16[3,32,256]{2,1,0:T(8,128)(2,1)S(1)}, u32[]{:S(2)}, u32[]{:S(2)}) collective-permute-start(bf16[3,32,256]{2,1,0:T(8,128)(2,1)S(1)} %collective-permute-done), channel_id=1, source_target_pairs={{0,2},{2,0},{1,3},{3,1},{4,6},{6,4},{5,7},{7,5},{8,10},{10,8},{9,1... | collective-permute-start | bytes 147464 | tf_op jit(solution)/shard_map/ppermute | solution.py:15
  16.1 4.1 %collective-permute-start.2 = (bf16[3,32,256]{2,1,0:T(8,128)(2,1)S(1)}, bf16[3,32,256]{2,1,0:T(8,128)(2,1)S(1)}, u32[]{:S(2)}, u32[]{:S(2)}) collective-permute-start(bf16[3,32,256]{2,1,0:T(8,128)(2,1)S(1)} %collective-permute-done.1), channel_id=1, source_target_pairs={{0,4},{4,0},{1,5},{5,1},{2,6},{6,2},{3,7},{7,3},{8,12},{12,8},{9,1... | collective-permute-start | bytes 147464 | tf_op jit(solution)/shard_map/ppermute | solution.py:15
  18.2 16.6 %copy-start.18 = (f32[1,1,256]{2,1,0:T(1,128)}, f32[1,1,256]{2,1,0:T(1,128)S(1)}, u32[]{:S(2)}) copy-start(f32[1,1,256]{2,1,0:T(1,128)S(1)} %get-tuple-element.113) | copy-start | bytes 3076
  18.2 16.6 %copy-start.20 = (f32[1,1,256]{2,1,0:T(1,128)}, f32[1,1,256]{2,1,0:T(1,128)S(1)}, u32[]{:S(2)}) copy-start(f32[1,1,256]{2,1,0:T(1,128)S(1)} %get-tuple-element.114) | copy-start | bytes 3076
  18.2 16.6 %copy-start.22 = (f32[1,1,256]{2,1,0:T(1,128)}, f32[1,1,256]{2,1,0:T(1,128)S(1)}, u32[]{:S(2)}) copy-start(f32[1,1,256]{2,1,0:T(1,128)S(1)} %get-tuple-element.115) | copy-start | bytes 3076
  18.2 16.6 %copy-start.24 = (f32[1,1,256]{2,1,0:T(1,128)}, f32[1,1,256]{2,1,0:T(1,128)S(1)}, u32[]{:S(2)}) copy-start(f32[1,1,256]{2,1,0:T(1,128)S(1)} %get-tuple-element.116) | copy-start | bytes 3076
  18.2 16.6 %copy-start.26 = (f32[1,1,256]{2,1,0:T(1,128)}, f32[1,1,256]{2,1,0:T(1,128)S(1)}, u32[]{:S(2)}) copy-start(f32[1,1,256]{2,1,0:T(1,128)S(1)} %get-tuple-element.117) | copy-start | bytes 3076
  18.3 16.6 %copy-start.28 = (f32[1,1,256]{2,1,0:T(1,128)}, f32[1,1,256]{2,1,0:T(1,128)S(1)}, u32[]{:S(2)}) copy-start(f32[1,1,256]{2,1,0:T(1,128)S(1)} %get-tuple-element.118) | copy-start | bytes 3076
  20.3 5.1 %collective-permute-start.3 = (bf16[3,32,256]{2,1,0:T(8,128)(2,1)S(1)}, bf16[3,32,256]{2,1,0:T(8,128)(2,1)S(1)}, u32[]{:S(2)}, u32[]{:S(2)}) collective-permute-start(bf16[3,32,256]{2,1,0:T(8,128)(2,1)S(1)} %collective-permute-done.2), channel_id=1, source_target_pairs={{0,8},{8,0},{1,9},{9,1},{2,10},{10,2},{3,11},{11,3},{4,12},{12,4},... | collective-permute-start | bytes 147464 | tf_op jit(solution)/shard_map/ppermute | solution.py:15
  23.9 11.0 %copy-start.30 = (f32[1,1,256]{2,1,0:T(1,128)}, f32[1,1,256]{2,1,0:T(1,128)S(1)}, u32[]{:S(2)}) copy-start(f32[1,1,256]{2,1,0:T(1,128)S(1)} %get-tuple-element.119) | copy-start | bytes 3076
  23.9 11.0 %copy-start.32 = (f32[1,1,256]{2,1,0:T(1,128)}, f32[1,1,256]{2,1,0:T(1,128)S(1)}, u32[]{:S(2)}) copy-start(f32[1,1,256]{2,1,0:T(1,128)S(1)} %get-tuple-element.120) | copy-start | bytes 3076
  23.9 11.0 %copy-start.34 = (f32[1,1,256]{2,1,0:T(1,128)}, f32[1,1,256]{2,1,0:T(1,128)S(1)}, u32[]{:S(2)}) copy-start(f32[1,1,256]{2,1,0:T(1,128)S(1)} %get-tuple-element.121) | copy-start | bytes 3076
  23.9 11.0 %copy-start.36 = (f32[1,1,256]{2,1,0:T(1,128)}, f32[1,1,256]{2,1,0:T(1,128)S(1)}, u32[]{:S(2)}) copy-start(f32[1,1,256]{2,1,0:T(1,128)S(1)} %get-tuple-element.122) | copy-start | bytes 3076
  23.9 11.0 %copy-start.38 = (f32[1,1,256]{2,1,0:T(1,128)}, f32[1,1,256]{2,1,0:T(1,128)S(1)}, u32[]{:S(2)}) copy-start(f32[1,1,256]{2,1,0:T(1,128)S(1)} %get-tuple-element.123) | copy-start | bytes 3076
  24.0 11.0 %copy-start.40 = (f32[1,1,256]{2,1,0:T(1,128)}, f32[1,1,256]{2,1,0:T(1,128)S(1)}, u32[]{:S(2)}) copy-start(f32[1,1,256]{2,1,0:T(1,128)S(1)} %get-tuple-element.124) | copy-start | bytes 3076
  24.0 11.0 %copy-start.42 = (f32[1,1,256]{2,1,0:T(1,128)}, f32[1,1,256]{2,1,0:T(1,128)S(1)}, u32[]{:S(2)}) copy-start(f32[1,1,256]{2,1,0:T(1,128)S(1)} %get-tuple-element.125) | copy-start | bytes 3076
  24.0 11.0 %copy-start.44 = (f32[1,1,256]{2,1,0:T(1,128)}, f32[1,1,256]{2,1,0:T(1,128)S(1)}, u32[]{:S(2)}) copy-start(f32[1,1,256]{2,1,0:T(1,128)S(1)} %get-tuple-element.126) | copy-start | bytes 3076
  24.0 11.0 %copy-start.46 = (f32[1,1,256]{2,1,0:T(1,128)}, f32[1,1,256]{2,1,0:T(1,128)S(1)}, u32[]{:S(2)}) copy-start(f32[1,1,256]{2,1,0:T(1,128)S(1)} %get-tuple-element.127) | copy-start | bytes 3076
  25.6 7.4 %collective-permute-start.4 = (bf16[70,3,256]{2,1,0:T(4,128)(2,1)S(1)}, bf16[70,3,256]{2,1,0:T(4,128)(2,1)S(1)}, u32[]{:S(2)}, u32[]{:S(2)}) collective-permute-start(bf16[70,3,256]{2,1,0:T(4,128)(2,1)S(1)} %get-tuple-element.96), channel_id=1, source_target_pairs={{0,1},{1,2},{2,3},{3,4},{4,5},{5,6},{6,7},{7,8},{8,9},{9,10},{10,1... | collective-permute-start | bytes 322568 | tf_op jit(solution)/shard_map/ppermute | solution.py:25
  25.6 7.3 %collective-permute-start.5 = (bf16[70,3,256]{2,1,0:T(4,128)(2,1)S(1)}, bf16[70,3,256]{2,1,0:T(4,128)(2,1)S(1)}, u32[]{:S(2)}, u32[]{:S(2)}) collective-permute-start(bf16[70,3,256]{2,1,0:T(4,128)(2,1)S(1)} %get-tuple-element.97), channel_id=1, source_target_pairs={{1,0},{2,1},{3,2},{4,3},{5,4},{6,5},{7,6},{8,7},{9,8},{10,9},{11,1... | collective-permute-start | bytes 322568 | tf_op jit(solution)/shard_map/ppermute | solution.py:27
  72.6 7.0 %copy-start.27 = (f32[1,1,256]{2,1,0:T(1,128)S(1)}, f32[1,1,256]{2,1,0:T(1,128)}, u32[]{:S(2)}) copy-start(f32[1,1,256]{2,1,0:T(1,128)} %copy-done.26) | copy-start | bytes 3076
  72.6 7.0 %copy-start.29 = (f32[1,1,256]{2,1,0:T(1,128)S(1)}, f32[1,1,256]{2,1,0:T(1,128)}, u32[]{:S(2)}) copy-start(f32[1,1,256]{2,1,0:T(1,128)} %copy-done.28) | copy-start | bytes 3076
  72.6 7.0 %copy-start.31 = (f32[1,1,256]{2,1,0:T(1,128)S(1)}, f32[1,1,256]{2,1,0:T(1,128)}, u32[]{:S(2)}) copy-start(f32[1,1,256]{2,1,0:T(1,128)} %copy-done.30) | copy-start | bytes 3076
  72.6 7.0 %copy-start.33 = (f32[1,1,256]{2,1,0:T(1,128)S(1)}, f32[1,1,256]{2,1,0:T(1,128)}, u32[]{:S(2)}) copy-start(f32[1,1,256]{2,1,0:T(1,128)} %copy-done.32) | copy-start | bytes 3076
  72.6 7.0 %copy-start.35 = (f32[1,1,256]{2,1,0:T(1,128)S(1)}, f32[1,1,256]{2,1,0:T(1,128)}, u32[]{:S(2)}) copy-start(f32[1,1,256]{2,1,0:T(1,128)} %copy-done.34) | copy-start | bytes 3076
  72.6 7.0 %copy-start.37 = (f32[1,1,256]{2,1,0:T(1,128)S(1)}, f32[1,1,256]{2,1,0:T(1,128)}, u32[]{:S(2)}) copy-start(f32[1,1,256]{2,1,0:T(1,128)} %copy-done.36) | copy-start | bytes 3076
  72.6 7.0 %copy-start.39 = (f32[1,1,256]{2,1,0:T(1,128)S(1)}, f32[1,1,256]{2,1,0:T(1,128)}, u32[]{:S(2)}) copy-start(f32[1,1,256]{2,1,0:T(1,128)} %copy-done.38) | copy-start | bytes 3076
  72.6 7.0 %copy-start.41 = (f32[1,1,256]{2,1,0:T(1,128)S(1)}, f32[1,1,256]{2,1,0:T(1,128)}, u32[]{:S(2)}) copy-start(f32[1,1,256]{2,1,0:T(1,128)} %copy-done.40) | copy-start | bytes 3076
  72.6 7.0 %copy-start.43 = (f32[1,1,256]{2,1,0:T(1,128)S(1)}, f32[1,1,256]{2,1,0:T(1,128)}, u32[]{:S(2)}) copy-start(f32[1,1,256]{2,1,0:T(1,128)} %copy-done.42) | copy-start | bytes 3076
  72.7 7.0 %copy-start.45 = (f32[1,1,256]{2,1,0:T(1,128)S(1)}, f32[1,1,256]{2,1,0:T(1,128)}, u32[]{:S(2)}) copy-start(f32[1,1,256]{2,1,0:T(1,128)} %copy-done.44) | copy-start | bytes 3076
  72.7 7.0 %copy-start.47 = (f32[1,1,256]{2,1,0:T(1,128)S(1)}, f32[1,1,256]{2,1,0:T(1,128)}, u32[]{:S(2)}) copy-start(f32[1,1,256]{2,1,0:T(1,128)} %copy-done.46) | copy-start | bytes 3076
  72.7 7.0 %copy-start.49 = (f32[1,1,256]{2,1,0:T(1,128)S(1)}, f32[1,1,256]{2,1,0:T(1,128)}, u32[]{:S(2)}) copy-start(f32[1,1,256]{2,1,0:T(1,128)} %get-tuple-element.128) | copy-start | bytes 3076
  72.7 7.0 %copy-start.51 = (f32[1,1,256]{2,1,0:T(1,128)S(1)}, f32[1,1,256]{2,1,0:T(1,128)}, u32[]{:S(2)}) copy-start(f32[1,1,256]{2,1,0:T(1,128)} %get-tuple-element.129) | copy-start | bytes 3076
  72.7 7.0 %copy-start.53 = (f32[1,1,256]{2,1,0:T(1,128)S(1)}, f32[1,1,256]{2,1,0:T(1,128)}, u32[]{:S(2)}) copy-start(f32[1,1,256]{2,1,0:T(1,128)} %get-tuple-element.130) | copy-start | bytes 3076
  72.7 7.0 %copy-start.55 = (f32[1,1,256]{2,1,0:T(1,128)S(1)}, f32[1,1,256]{2,1,0:T(1,128)}, u32[]{:S(2)}) copy-start(f32[1,1,256]{2,1,0:T(1,128)} %get-tuple-element.131) | copy-start | bytes 3076
  72.7 7.0 %copy-start.57 = (f32[1,1,256]{2,1,0:T(1,128)S(1)}, f32[1,1,256]{2,1,0:T(1,128)}, u32[]{:S(2)}) copy-start(f32[1,1,256]{2,1,0:T(1,128)} %get-tuple-element.132) | copy-start | bytes 3076
  72.7 7.0 %copy-start.59 = (f32[1,1,256]{2,1,0:T(1,128)S(1)}, f32[1,1,256]{2,1,0:T(1,128)}, u32[]{:S(2)}) copy-start(f32[1,1,256]{2,1,0:T(1,128)} %get-tuple-element.133) | copy-start | bytes 3076
  72.7 7.0 %copy-start.61 = (f32[1,1,256]{2,1,0:T(1,128)S(1)}, f32[1,1,256]{2,1,0:T(1,128)}, u32[]{:S(2)}) copy-start(f32[1,1,256]{2,1,0:T(1,128)} %get-tuple-element.134) | copy-start | bytes 3076
  72.7 7.0 %copy-start.63 = (f32[1,1,256]{2,1,0:T(1,128)S(1)}, f32[1,1,256]{2,1,0:T(1,128)}, u32[]{:S(2)}) copy-start(f32[1,1,256]{2,1,0:T(1,128)} %get-tuple-element.135) | copy-start | bytes 3076
  72.8 7.0 %copy-start.65 = (f32[1,1,256]{2,1,0:T(1,128)S(1)}, f32[1,1,256]{2,1,0:T(1,128)}, u32[]{:S(2)}) copy-start(f32[1,1,256]{2,1,0:T(1,128)} %get-tuple-element.136) | copy-start | bytes 3076
  72.8 7.0 %copy-start.67 = (f32[1,1,256]{2,1,0:T(1,128)S(1)}, f32[1,1,256]{2,1,0:T(1,128)}, u32[]{:S(2)}) copy-start(f32[1,1,256]{2,1,0:T(1,128)} %get-tuple-element.137) | copy-start | bytes 3076
  72.8 7.0 %copy-start.69 = (f32[1,1,256]{2,1,0:T(1,128)S(1)}, f32[1,1,256]{2,1,0:T(1,128)}, u32[]{:S(2)}) copy-start(f32[1,1,256]{2,1,0:T(1,128)} %copy-done.68) | copy-start | bytes 3076
  72.8 7.0 %copy-start.71 = (f32[1,1,256]{2,1,0:T(1,128)S(1)}, f32[1,1,256]{2,1,0:T(1,128)}, u32[]{:S(2)}) copy-start(f32[1,1,256]{2,1,0:T(1,128)} %copy-done.70) | copy-start | bytes 3076
  72.8 7.0 %copy-start.73 = (f32[1,1,256]{2,1,0:T(1,128)S(1)}, f32[1,1,256]{2,1,0:T(1,128)}, u32[]{:S(2)}) copy-start(f32[1,1,256]{2,1,0:T(1,128)} %copy-done.72) | copy-start | bytes 3076
  72.8 7.0 %copy-start.75 = (f32[1,1,256]{2,1,0:T(1,128)S(1)}, f32[1,1,256]{2,1,0:T(1,128)}, u32[]{:S(2)}) copy-start(f32[1,1,256]{2,1,0:T(1,128)} %copy-done.74) | copy-start | bytes 3076
  72.8 7.0 %copy-start.77 = (f32[1,1,256]{2,1,0:T(1,128)S(1)}, f32[1,1,256]{2,1,0:T(1,128)}, u32[]{:S(2)}) copy-start(f32[1,1,256]{2,1,0:T(1,128)} %copy-done.76) | copy-start | bytes 3076
  72.8 7.0 %copy-start.79 = (f32[1,1,256]{2,1,0:T(1,128)S(1)}, f32[1,1,256]{2,1,0:T(1,128)}, u32[]{:S(2)}) copy-start(f32[1,1,256]{2,1,0:T(1,128)} %copy-done.78) | copy-start | bytes 3076
  72.8 7.0 %copy-start.81 = (f32[1,1,256]{2,1,0:T(1,128)S(1)}, f32[1,1,256]{2,1,0:T(1,128)}, u32[]{:S(2)}) copy-start(f32[1,1,256]{2,1,0:T(1,128)} %copy-done.80) | copy-start | bytes 3076
  72.8 7.0 %copy-start.83 = (f32[1,1,256]{2,1,0:T(1,128)S(1)}, f32[1,1,256]{2,1,0:T(1,128)}, u32[]{:S(2)}) copy-start(f32[1,1,256]{2,1,0:T(1,128)} %copy-done.82) | copy-start | bytes 3076
  79.5 22.6 %copy-start.3 = (f32[64,32,256]{2,1,0:T(8,128)}, f32[64,32,256]{2,1,0:T(8,128)S(1)}, u32[]{:S(2)}) copy-start(f32[64,32,256]{2,1,0:T(8,128)S(1)} %get-tuple-element.89) | copy-start | bytes 6291460
  79.8 26.9 %copy-start.8 = (bf16[64,32,256]{2,1,0:T(8,128)(2,1)S(1)}, bf16[64,32,256]{2,1,0:T(8,128)(2,1)}, u32[]{:S(2)}) copy-start(bf16[64,32,256]{2,1,0:T(8,128)(2,1)} %copy-done.7) | copy-start | bytes 3145732
  102.2 10.8 %copy-start.10 = (bf16[70,3,256]{2,1,0:T(4,128)(2,1)}, bf16[70,3,256]{2,1,0:T(4,128)(2,1)S(1)}, u32[]{:S(2)}) copy-start(bf16[70,3,256]{2,1,0:T(4,128)(2,1)S(1)} %get-tuple-element.95) | copy-start | bytes 322564
  102.3 10.8 %collective-permute-start.6 = (bf16[70,3,256]{2,1,0:T(4,128)(2,1)S(1)}, bf16[70,3,256]{2,1,0:T(4,128)(2,1)S(1)}, u32[]{:S(2)}, u32[]{:S(2)}) collective-permute-start(bf16[70,3,256]{2,1,0:T(4,128)(2,1)S(1)} %get-tuple-element.94), channel_id=1, source_target_pairs={{0,1},{1,2},{2,3},{3,4},{4,5},{5,6},{6,7},{7,8},{8,9},{9,10},{10,1... | collective-permute-start | bytes 322568 | tf_op jit(solution)/shard_map/ppermute | solution.py:25
  103.0 10.1 %collective-permute-start.7 = (bf16[70,3,256]{2,1,0:T(4,128)(2,1)S(1)}, bf16[70,3,256]{2,1,0:T(4,128)(2,1)S(1)}, u32[]{:S(2)}, u32[]{:S(2)}) collective-permute-start(bf16[70,3,256]{2,1,0:T(4,128)(2,1)S(1)} %get-tuple-element.95), channel_id=1, source_target_pairs={{1,0},{2,1},{3,2},{4,3},{5,4},{6,5},{7,6},{8,7},{9,8},{10,9},{11,1... | collective-permute-start | bytes 322568 | tf_op jit(solution)/shard_map/ppermute | solution.py:27
  128.2 3.2 %collective-permute-start.8 = (bf16[3,32,256]{2,1,0:T(8,128)(2,1)S(1)}, bf16[3,32,256]{2,1,0:T(8,128)(2,1)}, u32[]{:S(2)}, u32[]{:S(2)}) collective-permute-start(bf16[3,32,256]{2,1,0:T(8,128)(2,1)S(1)} %slice.1409), channel_id=1, source_target_pairs={{0,1},{1,0},{2,3},{3,2},{4,5},{5,4},{6,7},{7,6},{8,9},{9,8},{10,11... | collective-permute-start | bytes 147464 | tf_op jit(solution)/shard_map/ppermute | solution.py:15
  131.5 6.4 %collective-permute-start.9 = (bf16[3,32,256]{2,1,0:T(8,128)(2,1)}, bf16[3,32,256]{2,1,0:T(8,128)(2,1)}, u32[]{:S(2)}, u32[]{:S(2)}) collective-permute-start(bf16[3,32,256]{2,1,0:T(8,128)(2,1)} %collective-permute-done.8), channel_id=1, source_target_pairs={{0,2},{2,0},{1,3},{3,1},{4,6},{6,4},{5,7},{7,5},{8,10},{10,8},{9,1... | collective-permute-start | bytes 147464 | tf_op jit(solution)/shard_map/ppermute | solution.py:15
  137.9 6.1 %collective-permute-start.10 = (bf16[3,32,256]{2,1,0:T(8,128)(2,1)}, bf16[3,32,256]{2,1,0:T(8,128)(2,1)}, u32[]{:S(2)}, u32[]{:S(2)}) collective-permute-start(bf16[3,32,256]{2,1,0:T(8,128)(2,1)} %collective-permute-done.9), channel_id=1, source_target_pairs={{0,4},{4,0},{1,5},{5,1},{2,6},{6,2},{3,7},{7,3},{8,12},{12,8},{9,1... | collective-permute-start | bytes 147464 | tf_op jit(solution)/shard_map/ppermute | solution.py:15
  144.0 65.4 %collective-permute-start.11 = (bf16[3,32,256]{2,1,0:T(8,128)(2,1)}, bf16[3,32,256]{2,1,0:T(8,128)(2,1)S(1)}, u32[]{:S(2)}, u32[]{:S(2)}) collective-permute-start(bf16[3,32,256]{2,1,0:T(8,128)(2,1)} %collective-permute-done.10), channel_id=1, source_target_pairs={{0,8},{8,0},{1,9},{9,1},{2,10},{10,2},{3,11},{11,3},{4,12},{12,4},... | collective-permute-start | bytes 147464 | tf_op jit(solution)/shard_map/ppermute | solution.py:15
  (60 other events, 279.5 us)
Sparse Core Ops, SparseCore 0:
  131.6 59.5 reduce-scatter.1
where the time goes:
time: 222 us; the launch traced here: 221 us
  other arithmetic  76.8 us (35%)
  blocking collectives  61.8 us (28%)
  local copies, waits for them, and re-layouts  21.1 us (10%)
  starting transfers between devices  19.4 us (9%)
  matrix products  18.8 us (8%)
  between operations  15.8 us (7%)
  waiting for transfers between devices  7.55 us (3%)
    psum x1, blocking collectives, local(): grad_kernel = lax.psum(local_kernel, 'lon')  61.8 us
    another operation x1, other arithmetic  22.2 us
    reduce_sum x3, other arithmetic, local(): jnp.sum(grad_conv * ext_wide[row_tap:row_tap + band_rows, col_tap:col_tap...  17.1 us
    reduce_sum x1, other arithmetic, local(): mean_z = jnp.mean(conv, axis=-1, keepdims=True)  15.9 us
    ppermute x8, starting transfers between devices, from_partner(): return lax.ppermute(block, axis, route)  10.4 us
    ppermute x2, starting transfers between devices, extended_2(): lax.ppermute(head, axis, [((i + 1) % count, i) for i in range(count)])  8.19 us
    dot_general x1, matrix products, local(): dhid = jnp.dot(dout, down_weight, preferred_element_type=jnp.float32)  6.25 us
    scatter-add x1, local copies, waits for them, and re-layouts, local(): grad_padded = grad_padded.at[:, :3].add(arrived[:, :3])  5.24 us
  transfers between devices with their start and end apart: 13, of which 5 were waited for; matrix products, arithmetic and copies ran while one was open for 13% of the time, Pallas kernels for 0%

commit v1 on v0

--- a/solution.py
+++ b/solution.py
@@ -107,7 +107,8 @@
                 )
             )
     local_kernel = jnp.stack(taps, axis=0).reshape(7, 7, channels) * factor
-    grad_kernel = lax.psum(local_kernel, "lon")
+    parts = lax.all_gather(local_kernel, "lon")
+    grad_kernel = jnp.sum(parts, axis=0)
     grad_pad = jnp.pad(grad_conv, ((6, 6), (6, 6), (0, 0)))
     grad_ext = jnp.zeros((band_rows + 6, band_cols + 6, channels), jnp.float32)
     for row_tap in range(7):

time: 222 us -> 190 us (0.86)
  blocking collectives: 61.8 us -> 23.7 us
  waiting for transfers between devices: 7.55 us -> 13.6 us
  other arithmetic: 76.8 us -> 79.5 us
  matrix products: 18.8 us -> 16.5 us
    psum x1 -> x0, blocking collectives: 61.8 us -> none  [local(): grad_kernel = lax.psum(local_kernel, 'lon')]
    all_gather x0 -> x1, blocking collectives: none -> 23.7 us  [local(): parts = lax.all_gather(local_kernel, 'lon')]
    ppermute x8, waiting for transfers between devices: 4.87 us -> 10.9 us  [from_partner(): return lax.ppermute(block, axis, route)]
    dot_general x1, matrix products: 4.53 us -> 2.26 us  [local(): lax.dot_general(normed, dpre, contract_rows, preferred_element_type=jnp.f...]
  transfers between devices with their start and end apart: 13 -> 13, of which waited for: 5 -> 6; matrix products, arithmetic and copies ran while one was open for 13% -> 22% of each run, Pallas kernels for 0% -> 0%
where the time goes in v1:
time: 190 us; the launch traced here: 189 us
  other arithmetic  79.5 us (42%)
  blocking collectives  23.7 us (12%)
  local copies, waits for them, and re-layouts  21.9 us (12%)
  starting transfers between devices  18.4 us (10%)
  matrix products  16.5 us (9%)
  between operations  15.7 us (8%)
  waiting for transfers between devices  13.6 us (7%)
    all_gather x1, blocking collectives, local(): parts = lax.all_gather(local_kernel, 'lon')  23.7 us
    another operation x1, other arithmetic  22.8 us
    reduce_sum x3, other arithmetic, local(): jnp.sum(grad_conv * ext_wide[row_tap:row_tap + band_rows, col_tap:col_tap...  17.2 us
    reduce_sum x1, other arithmetic, local(): mean_z = jnp.mean(conv, axis=-1, keepdims=True)  16.1 us
    ppermute x8, waiting for transfers between devices, from_partner(): return lax.ppermute(block, axis, route)  10.9 us
    ppermute x8, starting transfers between devices, from_partner(): return lax.ppermute(block, axis, route)  9.39 us
    ppermute x2, starting transfers between devices, extended_2(): lax.ppermute(head, axis, [((i + 1) % count, i) for i in range(count)])  8.19 us
    dot_general x1, matrix products, local(): dhid = jnp.dot(dout, down_weight, preferred_element_type=jnp.float32)  6.25 us
  transfers between devices with their start and end apart: 13, of which 6 were waited for; matrix products, arithmetic and copies ran while one was open for 22% of the time, Pallas kernels for 0%

profile of v1, /device:TPU:0, one launch (start us, length us, event | category | flops | bytes accessed | tf_op | source)
XLA Modules:
  0.0 189.4 jit_solution(9124217590220330203)
XLA Ops:
  7.2 0.0 copy-start
  7.2 0.0 copy-start.8
  7.2 0.0 reduce-scatter.2.cloned.1.call-start
  7.2 0.8 convert_element_type.47
  8.1 0.1 copy.17
  8.2 1.6 broadcast_multiply_fusion
  9.8 0.5 collective-permute-start
  10.3 0.1 copy.16
  10.4 0.8 collective-permute-done
  11.2 2.9 %collective-permute-start.1 = (bf16[3,32,256]{2,1,0:T(8,128)(2,1)S(1)}, bf16[3,32,256]{2,1,0:T(8,128)(2,1)S(1)}, u32[]{:S(2)}, u32[]{:S(2)}) collective-permute-start(bf16[3,32,256]{2,1,0:T(8,128)(2,1)S(1)} %collective-permute-done), channel_id=1, source_target_pairs={{0,2},{2,0},{1,3},{3,1},{4,6},{6,4},{5,7},{7,5},{8,10},{10,8},{9,1... | collective-permute-start | bytes 147464 | tf_op jit(solution)/shard_map/ppermute | solution.py:15
  14.0 1.3 fusion.106
  15.4 0.7 collective-permute-done.1
  16.1 2.1 %collective-permute-start.2 = (bf16[3,32,256]{2,1,0:T(8,128)(2,1)S(1)}, bf16[3,32,256]{2,1,0:T(8,128)(2,1)S(1)}, u32[]{:S(2)}, u32[]{:S(2)}) collective-permute-start(bf16[3,32,256]{2,1,0:T(8,128)(2,1)S(1)} %collective-permute-done.1), channel_id=1, source_target_pairs={{0,4},{4,0},{1,5},{5,1},{2,6},{6,2},{3,7},{7,3},{8,12},{12,8},{9,1... | collective-permute-start | bytes 147464 | tf_op jit(solution)/shard_map/ppermute | solution.py:15
  18.3 2.0 %collective-permute-done.2 = bf16[3,32,256]{2,1,0:T(8,128)(2,1)S(1)} collective-permute-done((bf16[3,32,256]{2,1,0:T(8,128)(2,1)S(1)}, bf16[3,32,256]{2,1,0:T(8,128)(2,1)S(1)}, u32[]{:S(2)}, u32[]{:S(2)}) %collective-permute-start.2) | collective-permute-done | bytes 49184 | tf_op jit(solution)/shard_map/ppermute | solution.py:15
  20.3 3.0 %collective-permute-start.3 = (bf16[3,32,256]{2,1,0:T(8,128)(2,1)S(1)}, bf16[3,32,256]{2,1,0:T(8,128)(2,1)S(1)}, u32[]{:S(2)}, u32[]{:S(2)}) collective-permute-start(bf16[3,32,256]{2,1,0:T(8,128)(2,1)S(1)} %collective-permute-done.2), channel_id=1, source_target_pairs={{0,8},{8,0},{1,9},{9,1},{2,10},{10,2},{3,11},{11,3},{4,12},{12,4},... | collective-permute-start | bytes 147464 | tf_op jit(solution)/shard_map/ppermute | solution.py:15
  23.3 0.6 fusion.119
  24.0 1.4 collective-permute-done.3
  25.4 0.1 rev.6
  25.5 0.1 pad_maximum_fusion.5
  25.6 0.1 collective-permute-start.4
  25.6 4.4 %collective-permute-start.5 = (bf16[70,3,256]{2,1,0:T(4,128)(2,1)S(1)}, bf16[70,3,256]{2,1,0:T(4,128)(2,1)S(1)}, u32[]{:S(2)}, u32[]{:S(2)}) collective-permute-start(bf16[70,3,256]{2,1,0:T(4,128)(2,1)S(1)} %get-tuple-element.97), channel_id=1, source_target_pairs={{1,0},{2,1},{3,2},{4,3},{5,4},{6,5},{7,6},{8,7},{9,8},{10,9},{11,1... | collective-permute-start | bytes 322568 | tf_op jit(solution)/shard_map/ppermute | solution.py:27
  30.2 0.0 copy-start.86
  30.3 2.7 %collective-permute-done.4 = bf16[70,3,256]{2,1,0:T(4,128)(2,1)S(1)} collective-permute-done((bf16[70,3,256]{2,1,0:T(4,128)(2,1)S(1)}, bf16[70,3,256]{2,1,0:T(4,128)(2,1)S(1)}, u32[]{:S(2)}, u32[]{:S(2)}) %collective-permute-start.4) | collective-permute-done | bytes 107552 | tf_op jit(solution)/shard_map/ppermute | solution.py:25
  33.0 1.9 maximum_convert_fusion
  35.2 16.1 %fusion.115 = (f32[64,32]{1,0:T(8,128)S(1)}, f32[64,32,256]{2,1,0:T(8,128)}) fusion(f32[70,38,256]{2,1,0:T(8,128)S(1)} %maximum_convert_fusion, f32[256]{0:T(256)S(1)} %bitcast.211, f32[256]{0:T(256)S(1)} %bitcast.213, f32[256]{0:T(256)S(1)} %bitcast.119, f32[256]{0:T(256)S(1)} %bitcast.121, f32[256]{0:T(256)S(1)} %bitcast.123, f32[256]{0:T(256)S(1)} %bitcast.125, ...), kind=kLoop, calls=%fused_computation.242 | loop fusion | flops 51378176 | bytes 104915968 | tf_op jit(solution)/shard_map/reduce_sum | solution.py:62
  51.3 2.4 %multiply_reduce_fusion.51 = f32[64,32]{1,0:T(8,128)S(1)} fusion(f32[64,32,256]{2,1,0:T(8,128)} %get-tuple-element.93, f32[64,32]{1,0:T(8,128)S(1)} %broadcast_multiply_fusion.3), kind=kLoop, calls=%fused_computation.216 | loop fusion | flops 1570816 | bytes 2113536 | tf_op jit(solution)/shard_map/reduce_sum | solution.py:64
  53.7 0.7 multiply_convert_fusion.2
  54.5 1.3 fusion.121
  55.7 0.0 copy-start.107
  55.7 4.2 %fusion.7 = f32[256,1024]{1,0:T(8,128)} fusion(bf16[2048,256]{1,0:T(8,128)(2,1)S(1)} %bitcast.115, f32[2048,1024]{1,0:T(8,128)S(1)} %fusion.121), kind=kOutput, calls=%fused_computation.59 | convolution fusion | flops 1092616192 | bytes 10485760 | tf_op jit(solution)/shard_map/dot_general | solution.py:83
  59.9 6.3 %fusion.6 = bf16[2048,1024]{1,0:T(8,128)(2,1)S(1)} fusion(f32[2048,1024]{1,0:T(8,128)S(1)} %fusion.121, bf16[2048,256]{1,0:T(8,128)(2,1)S(1)} %bitcast.116, bf16[256,1024]{1,0:T(8,128)(2,1)S(1)} %copy-done.107), kind=kOutput, calls=%fused_computation.57 | convolution fusion | flops 1115684864 | bytes 14155776 | tf_op jit(solution)/shard_map/dot_general | solution.py:75
  66.2 2.3 %fusion.122 = f32[256,1024]{1,0:T(8,128)} fusion(bf16[2048,256]{1,0:T(8,128)(2,1)S(1)} %bitcast.114, bf16[2048,1024]{1,0:T(8,128)(2,1)S(1)} %fusion.6), kind=kOutput, calls=%fused_computation.249 | convolution fusion | flops 1073741824 | bytes 6291456 | tf_op jit(solution)/shard_map/dot_general | solution.py:82
  68.4 2.6 %multiply_reduce_fusion.50 = (f32[2048]{0:T(1024)S(1)}, f32[2048,256]{1,0:T(8,128)}) fusion(f32[256]{0:T(256)S(1)} %copy-done.15, bf16[2048,1024]{1,0:T(8,128)(2,1)S(1)} %fusion.6, bf16[256,1024]{1,0:T(8,128)(2,1)S(1)} %copy-done), kind=kOutput, calls=%fused_computation.214 | convolution fusion | flops 1074788352 | bytes 6824960 | tf_op jit(solution)/shard_map/dot_general | solution.py:92
  71.0 0.1 div.17
  71.1 2.9 %multiply_reduce_fusion.49 = f32[64,32]{1,0:T(8,128)S(1)} fusion(f32[64,32,256]{2,1,0:T(8,128)} %bitcast.112, f32[64,32,256]{2,1,0:T(8,128)} %get-tuple-element.93, f32[256]{0:T(256)S(1)} %copy-done.15, f32[64,32]{1,0:T(8,128)S(1)} %add_rsqrt_fusion, f32[64,32]{1,0:T(8,128)S(1)} %broadcast_multiply_fusion.3), kind=kLoop, calls=%fused_computation.213 | loop fusion | flops 2619392 | bytes 4219904 | tf_op jit(solution)/shard_map/reduce_sum | solution.py:97
  74.1 0.5 copy-done.7
  74.9 6.7 %multiply_reduce_fusion = (f32[256]{0:T(256)}, f32[256]{0:T(256)}, f32[256]{0:T(256)}, f32[256]{0:T(256)}, f32[256]{0:T(256)}, /*index=5*/f32[256]{0:T(256)}, f3...) fusion(f32[70,38,256]{2,1,0:T(8,128)S(1)} %maximum_convert_fusi, ...), kind=kLoop, calls=%fused_computation.163 | loop fusion | flops 22539776 | bytes 44092416 | tf_op jit(solution)/shard_map/reduce_sum | solution.py:103
  82.0 22.8 %fusion.113 = (bf16[70,38,256]{2,1,0:T(8,128)(2,1)S(1)}, f32[70,38,256]{2,1,0:T(8,128)}) fusion(f32[256]{0:T(256)S(1)} %bitcast.212, f32[256]{0:T(256)S(1)} %bitcast.214, f32[256]{0:T(256)S(1)} %bitcast.120, f32[256]{0:T(256)S(1)} %bitcast.122, f32[256]{0:T(256)S(1)} %bitcast.124, f32[256]{0:T(256)S(1)} %bitcast.126, f32[256]{0:T(256)S(1)} %bitcast.128, ...), kind=kLoop, calls=%fused_computation.241 | loop fusion | flops 66734080 | bytes 6233088 | tf_op jit(solution)/shard_map/convert.3
  104.8 0.8 fusion.116
  105.6 0.7 collective-permute-start.6
  106.2 3.8 %collective-permute-start.7 = (bf16[70,3,256]{2,1,0:T(4,128)(2,1)}, bf16[70,3,256]{2,1,0:T(4,128)(2,1)}, u32[]{:S(2)}, u32[]{:S(2)}) collective-permute-start(bf16[70,3,256]{2,1,0:T(4,128)(2,1)} %get-tuple-element.95), channel_id=1, source_target_pairs={{1,0},{2,1},{3,2},{4,3},{5,4},{6,5},{7,6},{8,7},{9,8},{10,9},{11,1... | collective-permute-start | bytes 322568 | tf_op jit(solution)/shard_map/ppermute | solution.py:27
  110.0 1.6 maximum_multiply_fusion
  111.6 0.0 reduce-scatter.2.cloned.1.call-update
  111.6 3.6 %slice.866 = f32[70,32,256]{2,1,0:T(8,128)} slice(f32[70,38,256]{2,1,0:T(8,128)} %get-tuple-element.91), slice={[0:70], [3:35], [0:256]} | slice | bytes 4587520 | tf_op jit(solution)/shard_map/slice | solution.py:125
  115.2 2.2 %convert_add_fusion.1 = f32[70,3,256]{2,1,0:T(4,128)} fusion(f32[70,38,256]{2,1,0:T(8,128)} %get-tuple-element.91, bf16[70,3,256]{2,1,0:T(4,128)(2,1)} %collective-permute-done.7, bf16[70,3,256]{2,1,0:T(4,128)(2,1)S(1)} %get-tuple-element.94, bf16[70,3,256]{2,1,0:T(4,128)(2,1)} %get-tuple-element.95, bf16[70,3,256]{2,1,0:T(4,128)(2,1)} %collective-permute-done.6), kind=kLoop, calls=%fused_computation.222 | loop fusion | flops 483840 | bytes 860160 | tf_op jit(solution)/shard_map/add | solution.py:126
  117.5 5.3 %scatter-add.10 = f32[70,32,256]{2,1,0:T(8,128)} dynamic-update-slice(f32[70,32,256]{2,1,0:T(8,128)} %slice.866, f32[70,3,256]{2,1,0:T(4,128)} %convert_add_fusion.1, s32[]{:T(128)} %constant.108.clone.1, s32[]{:T(128)} %constant.108.clone.1, s32[]{:T(128)} %constant.108.clone.1) | dynamic-update-slice | bytes 430084 | tf_op jit(solution)/shard_map/scatter-add | solution.py:126
  122.7 2.2 %slice_add_fusion = f32[70,3,256]{2,1,0:T(4,128)} fusion(f32[70,32,256]{2,1,0:T(8,128)} %scatter-add.10, bf16[70,3,256]{2,1,0:T(4,128)(2,1)} %collective-permute-done.7, bf16[70,3,256]{2,1,0:T(4,128)(2,1)S(1)} %get-tuple-element.94, bf16[70,3,256]{2,1,0:T(4,128)(2,1)} %get-tuple-element.95, bf16[70,3,256]{2,1,0:T(4,128)(2,1)} %collective-permute-done.6), kind=kLoop, calls=%fused_computation.221 | loop fusion | flops 483840 | bytes 860160 | tf_op jit(solution)/shard_map/add | solution.py:127
  124.9 4.6 %scatter-add.11 = f32[70,32,256]{2,1,0:T(8,128)} dynamic-update-slice(f32[70,32,256]{2,1,0:T(8,128)} %scatter-add.10, f32[70,3,256]{2,1,0:T(4,128)} %slice_add_fusion, s32[]{:T(128)} %constant.108.clone.1, s32[]{:T(128)} %constant.109.clone.1, s32[]{:T(128)} %constant.108.clone.1) | dynamic-update-slice | bytes 430084 | tf_op jit(solution)/shard_map/scatter-add | solution.py:127
  129.5 0.9 slice.1409
  130.4 0.1 collective-permute-start.8
  130.5 6.1 %multiply_reduce_fusion.18 = (f32[256]{0:T(256)S(1)}, f32[256]{0:T(256)S(1)}, f32[256]{0:T(256)S(1)}, f32[256]{0:T(256)S(1)}, f32[256]{0:T(256)S(1)}, /*index=5*...) fusion(f32[64,32,256]{2,1,0:T(8,128)} %copy-done.3, ...), kind=kLoop, calls=%fused_computation.181 | loop fusion | flops 18869760 | bytes 39864320 | tf_op jit(solution)/shard_map/reduce_sum | solution.py:103
  136.8 0.1 collective-permute-start.9
  136.9 4.3 %multiply_reduce_fusion.36 = (f32[256]{0:T(256)S(1)}, f32[256]{0:T(256)S(1)}, f32[256]{0:T(256)S(1)}, f32[256]{0:T(256)S(1)}, f32[256]{0:T(256)}, /*index=5*/f32...) fusion(f32[64,32,256]{2,1,0:T(8,128)S(1)} %copy-done.4, ...), kind=kLoop, calls=%fused_computation.199 | loop fusion | flops 13628160 | bytes 29373440 | tf_op jit(solution)/shard_map/reduce_sum | solution.py:103
  141.4 1.7 stack.199
  143.1 0.1 collective-permute-start.10
  143.2 6.0 %collective-permute-done.10 = bf16[3,32,256]{2,1,0:T(8,128)(2,1)S(1)} collective-permute-done((bf16[3,32,256]{2,1,0:T(8,128)(2,1)}, bf16[3,32,256]{2,1,0:T(8,128)(2,1)S(1)}, u32[]{:S(2)}, u32[]{:S(2)}) %collective-permute-start.10) | collective-permute-done | bytes 49184 | tf_op jit(solution)/shard_map/ppermute | solution.py:15
  149.2 0.7 collective-permute-start.11
  149.9 23.7 %all_gather.4 = f32[16,7,7,256]{3,2,1,0:T(8,128)} all-gather(f32[1,7,7,256]{3,2,1,0:T(8,128)S(1)} %mul.1504), channel_id=1, replica_groups=mesh['groups'=2,'lon'=16] {'lon'}, dimensions={0}, use_global_device_ids=true | all-gather | bytes 852992 | tf_op jit(solution)/shard_map/all_gather | solution.py:110
  173.7 1.9 reduce_sum.539
  175.5 1.5 slice.871
  177.0 0.1 rev.7
  177.1 0.6 fusion.108
  177.8 3.2 %fusion.107 = bf16[64,32,256]{2,1,0:T(8,128)(2,1)} fusion(bf16[64,32,256]{2,1,0:T(8,128)(2,1)} %param.16, f32[64,32,256]{2,1,0:T(8,128)} %fusion.108, f32[64,32]{1,0:T(8,128)S(1)} %copy-done.13), kind=kLoop, calls=%fused_computation.161 | loop fusion | flops 2097152 | bytes 4202496 | tf_op jit(solution)/shard_map/convert_element_type | solution.py:138
  181.0 1.5 fusion.117
  (228 shorter events, 0.5 us)
Async XLA Ops:
  7.2 47.3 %copy-start = (bf16[256,1024]{1,0:T(8,128)(2,1)S(1)}, bf16[256,1024]{1,0:T(8,128)(2,1)}, u32[]{:S(2)}) copy-start(bf16[256,1024]{1,0:T(8,128)(2,1)} %param.19) | copy-start | bytes 1572868
  7.2 173.8 %reduce-scatter.2.cloned.1.call-start = ((), (), s32[]{:S(2)}) async-start(), calls=%async_computation.1 | async-start | bytes 2228224 | tf_op jit(solution)/shard_map/reduce_scatter | solution.py:84
  8.2 10.0 %copy-start.14 = (f32[7,7,256]{2,1,0:T(8,128)S(1)}, f32[7,7,256]{2,1,0:T(8,128)}, u32[]{:S(2)}) copy-start(f32[7,7,256]{2,1,0:T(8,128)} %param.17) | copy-start | bytes 150532
  9.8 23.2 %copy-start.6 = (bf16[64,32,256]{2,1,0:T(8,128)(2,1)}, bf16[64,32,256]{2,1,0:T(8,128)(2,1)S(1)}, u32[]{:S(2)}) copy-start(bf16[64,32,256]{2,1,0:T(8,128)(2,1)S(1)} %broadcast_multiply_fusion) | copy-start | bytes 3145732
  9.8 1.4 collective-permute-start
  10.4 22.6 %copy-start.12 = (f32[64,32]{1,0:T(8,128)}, f32[64,32]{1,0:T(8,128)S(1)}, u32[]{:S(2)}) copy-start(f32[64,32]{1,0:T(8,128)S(1)} %copy.16) | copy-start | bytes 24580
  11.2 4.9 %collective-permute-start.1 = (bf16[3,32,256]{2,1,0:T(8,128)(2,1)S(1)}, bf16[3,32,256]{2,1,0:T(8,128)(2,1)S(1)}, u32[]{:S(2)}, u32[]{:S(2)}) collective-permute-start(bf16[3,32,256]{2,1,0:T(8,128)(2,1)S(1)} %collective-permute-done), channel_id=1, source_target_pairs={{0,2},{2,0},{1,3},{3,1},{4,6},{6,4},{5,7},{7,5},{8,10},{10,8},{9,1... | collective-permute-start | bytes 147464 | tf_op jit(solution)/shard_map/ppermute | solution.py:15
  16.1 4.1 %collective-permute-start.2 = (bf16[3,32,256]{2,1,0:T(8,128)(2,1)S(1)}, bf16[3,32,256]{2,1,0:T(8,128)(2,1)S(1)}, u32[]{:S(2)}, u32[]{:S(2)}) collective-permute-start(bf16[3,32,256]{2,1,0:T(8,128)(2,1)S(1)} %collective-permute-done.1), channel_id=1, source_target_pairs={{0,4},{4,0},{1,5},{5,1},{2,6},{6,2},{3,7},{7,3},{8,12},{12,8},{9,1... | collective-permute-start | bytes 147464 | tf_op jit(solution)/shard_map/ppermute | solution.py:15
  18.2 16.6 %copy-start.16 = (f32[1,1,256]{2,1,0:T(1,128)}, f32[1,1,256]{2,1,0:T(1,128)S(1)}, u32[]{:S(2)}) copy-start(f32[1,1,256]{2,1,0:T(1,128)S(1)} %get-tuple-element.113) | copy-start | bytes 3076
  18.2 16.6 %copy-start.18 = (f32[1,1,256]{2,1,0:T(1,128)}, f32[1,1,256]{2,1,0:T(1,128)S(1)}, u32[]{:S(2)}) copy-start(f32[1,1,256]{2,1,0:T(1,128)S(1)} %get-tuple-element.114) | copy-start | bytes 3076
  18.2 16.6 %copy-start.20 = (f32[1,1,256]{2,1,0:T(1,128)}, f32[1,1,256]{2,1,0:T(1,128)S(1)}, u32[]{:S(2)}) copy-start(f32[1,1,256]{2,1,0:T(1,128)S(1)} %get-tuple-element.115) | copy-start | bytes 3076
  18.2 16.6 %copy-start.22 = (f32[1,1,256]{2,1,0:T(1,128)}, f32[1,1,256]{2,1,0:T(1,128)S(1)}, u32[]{:S(2)}) copy-start(f32[1,1,256]{2,1,0:T(1,128)S(1)} %get-tuple-element.116) | copy-start | bytes 3076
  18.2 16.6 %copy-start.24 = (f32[1,1,256]{2,1,0:T(1,128)}, f32[1,1,256]{2,1,0:T(1,128)S(1)}, u32[]{:S(2)}) copy-start(f32[1,1,256]{2,1,0:T(1,128)S(1)} %get-tuple-element.117) | copy-start | bytes 3076
  18.3 16.6 %copy-start.26 = (f32[1,1,256]{2,1,0:T(1,128)}, f32[1,1,256]{2,1,0:T(1,128)S(1)}, u32[]{:S(2)}) copy-start(f32[1,1,256]{2,1,0:T(1,128)S(1)} %get-tuple-element.118) | copy-start | bytes 3076
  20.3 5.1 %collective-permute-start.3 = (bf16[3,32,256]{2,1,0:T(8,128)(2,1)S(1)}, bf16[3,32,256]{2,1,0:T(8,128)(2,1)S(1)}, u32[]{:S(2)}, u32[]{:S(2)}) collective-permute-start(bf16[3,32,256]{2,1,0:T(8,128)(2,1)S(1)} %collective-permute-done.2), channel_id=1, source_target_pairs={{0,8},{8,0},{1,9},{9,1},{2,10},{10,2},{3,11},{11,3},{4,12},{12,4},... | collective-permute-start | bytes 147464 | tf_op jit(solution)/shard_map/ppermute | solution.py:15
  23.9 11.0 %copy-start.28 = (f32[1,1,256]{2,1,0:T(1,128)}, f32[1,1,256]{2,1,0:T(1,128)S(1)}, u32[]{:S(2)}) copy-start(f32[1,1,256]{2,1,0:T(1,128)S(1)} %get-tuple-element.119) | copy-start | bytes 3076
  23.9 11.0 %copy-start.30 = (f32[1,1,256]{2,1,0:T(1,128)}, f32[1,1,256]{2,1,0:T(1,128)S(1)}, u32[]{:S(2)}) copy-start(f32[1,1,256]{2,1,0:T(1,128)S(1)} %get-tuple-element.120) | copy-start | bytes 3076
  23.9 11.0 %copy-start.32 = (f32[1,1,256]{2,1,0:T(1,128)}, f32[1,1,256]{2,1,0:T(1,128)S(1)}, u32[]{:S(2)}) copy-start(f32[1,1,256]{2,1,0:T(1,128)S(1)} %get-tuple-element.121) | copy-start | bytes 3076
  23.9 11.0 %copy-start.34 = (f32[1,1,256]{2,1,0:T(1,128)}, f32[1,1,256]{2,1,0:T(1,128)S(1)}, u32[]{:S(2)}) copy-start(f32[1,1,256]{2,1,0:T(1,128)S(1)} %get-tuple-element.122) | copy-start | bytes 3076
  23.9 11.0 %copy-start.36 = (f32[1,1,256]{2,1,0:T(1,128)}, f32[1,1,256]{2,1,0:T(1,128)S(1)}, u32[]{:S(2)}) copy-start(f32[1,1,256]{2,1,0:T(1,128)S(1)} %get-tuple-element.123) | copy-start | bytes 3076
  24.0 11.0 %copy-start.38 = (f32[1,1,256]{2,1,0:T(1,128)}, f32[1,1,256]{2,1,0:T(1,128)S(1)}, u32[]{:S(2)}) copy-start(f32[1,1,256]{2,1,0:T(1,128)S(1)} %get-tuple-element.124) | copy-start | bytes 3076
  24.0 11.0 %copy-start.40 = (f32[1,1,256]{2,1,0:T(1,128)}, f32[1,1,256]{2,1,0:T(1,128)S(1)}, u32[]{:S(2)}) copy-start(f32[1,1,256]{2,1,0:T(1,128)S(1)} %get-tuple-element.125) | copy-start | bytes 3076
  24.0 11.0 %copy-start.42 = (f32[1,1,256]{2,1,0:T(1,128)}, f32[1,1,256]{2,1,0:T(1,128)S(1)}, u32[]{:S(2)}) copy-start(f32[1,1,256]{2,1,0:T(1,128)S(1)} %get-tuple-element.126) | copy-start | bytes 3076
  24.0 11.0 %copy-start.44 = (f32[1,1,256]{2,1,0:T(1,128)}, f32[1,1,256]{2,1,0:T(1,128)S(1)}, u32[]{:S(2)}) copy-start(f32[1,1,256]{2,1,0:T(1,128)S(1)} %get-tuple-element.127) | copy-start | bytes 3076
  25.6 7.4 %collective-permute-start.4 = (bf16[70,3,256]{2,1,0:T(4,128)(2,1)S(1)}, bf16[70,3,256]{2,1,0:T(4,128)(2,1)S(1)}, u32[]{:S(2)}, u32[]{:S(2)}) collective-permute-start(bf16[70,3,256]{2,1,0:T(4,128)(2,1)S(1)} %get-tuple-element.96), channel_id=1, source_target_pairs={{0,1},{1,2},{2,3},{3,4},{4,5},{5,6},{6,7},{7,8},{8,9},{9,10},{10,1... | collective-permute-start | bytes 322568 | tf_op jit(solution)/shard_map/ppermute | solution.py:25
  25.6 7.3 %collective-permute-start.5 = (bf16[70,3,256]{2,1,0:T(4,128)(2,1)S(1)}, bf16[70,3,256]{2,1,0:T(4,128)(2,1)S(1)}, u32[]{:S(2)}, u32[]{:S(2)}) collective-permute-start(bf16[70,3,256]{2,1,0:T(4,128)(2,1)S(1)} %get-tuple-element.97), channel_id=1, source_target_pairs={{1,0},{2,1},{3,2},{4,3},{5,4},{6,5},{7,6},{8,7},{9,8},{10,9},{11,1... | collective-permute-start | bytes 322568 | tf_op jit(solution)/shard_map/ppermute | solution.py:27
  74.6 7.0 %copy-start.25 = (f32[1,1,256]{2,1,0:T(1,128)S(1)}, f32[1,1,256]{2,1,0:T(1,128)}, u32[]{:S(2)}) copy-start(f32[1,1,256]{2,1,0:T(1,128)} %copy-done.24) | copy-start | bytes 3076
  74.6 7.0 %copy-start.27 = (f32[1,1,256]{2,1,0:T(1,128)S(1)}, f32[1,1,256]{2,1,0:T(1,128)}, u32[]{:S(2)}) copy-start(f32[1,1,256]{2,1,0:T(1,128)} %copy-done.26) | copy-start | bytes 3076
  74.6 7.0 %copy-start.29 = (f32[1,1,256]{2,1,0:T(1,128)S(1)}, f32[1,1,256]{2,1,0:T(1,128)}, u32[]{:S(2)}) copy-start(f32[1,1,256]{2,1,0:T(1,128)} %copy-done.28) | copy-start | bytes 3076
  74.6 7.0 %copy-start.31 = (f32[1,1,256]{2,1,0:T(1,128)S(1)}, f32[1,1,256]{2,1,0:T(1,128)}, u32[]{:S(2)}) copy-start(f32[1,1,256]{2,1,0:T(1,128)} %copy-done.30) | copy-start | bytes 3076
  74.6 7.0 %copy-start.33 = (f32[1,1,256]{2,1,0:T(1,128)S(1)}, f32[1,1,256]{2,1,0:T(1,128)}, u32[]{:S(2)}) copy-start(f32[1,1,256]{2,1,0:T(1,128)} %copy-done.32) | copy-start | bytes 3076
  74.7 7.0 %copy-start.35 = (f32[1,1,256]{2,1,0:T(1,128)S(1)}, f32[1,1,256]{2,1,0:T(1,128)}, u32[]{:S(2)}) copy-start(f32[1,1,256]{2,1,0:T(1,128)} %copy-done.34) | copy-start | bytes 3076
  74.7 7.0 %copy-start.37 = (f32[1,1,256]{2,1,0:T(1,128)S(1)}, f32[1,1,256]{2,1,0:T(1,128)}, u32[]{:S(2)}) copy-start(f32[1,1,256]{2,1,0:T(1,128)} %copy-done.36) | copy-start | bytes 3076
  74.7 7.0 %copy-start.39 = (f32[1,1,256]{2,1,0:T(1,128)S(1)}, f32[1,1,256]{2,1,0:T(1,128)}, u32[]{:S(2)}) copy-start(f32[1,1,256]{2,1,0:T(1,128)} %copy-done.38) | copy-start | bytes 3076
  74.7 7.0 %copy-start.41 = (f32[1,1,256]{2,1,0:T(1,128)S(1)}, f32[1,1,256]{2,1,0:T(1,128)}, u32[]{:S(2)}) copy-start(f32[1,1,256]{2,1,0:T(1,128)} %copy-done.40) | copy-start | bytes 3076
  74.7 7.0 %copy-start.43 = (f32[1,1,256]{2,1,0:T(1,128)S(1)}, f32[1,1,256]{2,1,0:T(1,128)}, u32[]{:S(2)}) copy-start(f32[1,1,256]{2,1,0:T(1,128)} %copy-done.42) | copy-start | bytes 3076
  74.7 7.0 %copy-start.45 = (f32[1,1,256]{2,1,0:T(1,128)S(1)}, f32[1,1,256]{2,1,0:T(1,128)}, u32[]{:S(2)}) copy-start(f32[1,1,256]{2,1,0:T(1,128)} %copy-done.44) | copy-start | bytes 3076
  74.7 7.0 %copy-start.47 = (f32[1,1,256]{2,1,0:T(1,128)S(1)}, f32[1,1,256]{2,1,0:T(1,128)}, u32[]{:S(2)}) copy-start(f32[1,1,256]{2,1,0:T(1,128)} %get-tuple-element.128) | copy-start | bytes 3076
  74.7 7.0 %copy-start.49 = (f32[1,1,256]{2,1,0:T(1,128)S(1)}, f32[1,1,256]{2,1,0:T(1,128)}, u32[]{:S(2)}) copy-start(f32[1,1,256]{2,1,0:T(1,128)} %get-tuple-element.129) | copy-start | bytes 3076
  74.7 7.0 %copy-start.51 = (f32[1,1,256]{2,1,0:T(1,128)S(1)}, f32[1,1,256]{2,1,0:T(1,128)}, u32[]{:S(2)}) copy-start(f32[1,1,256]{2,1,0:T(1,128)} %get-tuple-element.130) | copy-start | bytes 3076
  74.7 7.0 %copy-start.53 = (f32[1,1,256]{2,1,0:T(1,128)S(1)}, f32[1,1,256]{2,1,0:T(1,128)}, u32[]{:S(2)}) copy-start(f32[1,1,256]{2,1,0:T(1,128)} %get-tuple-element.131) | copy-start | bytes 3076
  74.8 7.0 %copy-start.55 = (f32[1,1,256]{2,1,0:T(1,128)S(1)}, f32[1,1,256]{2,1,0:T(1,128)}, u32[]{:S(2)}) copy-start(f32[1,1,256]{2,1,0:T(1,128)} %get-tuple-element.132) | copy-start | bytes 3076
  74.8 7.0 %copy-start.57 = (f32[1,1,256]{2,1,0:T(1,128)S(1)}, f32[1,1,256]{2,1,0:T(1,128)}, u32[]{:S(2)}) copy-start(f32[1,1,256]{2,1,0:T(1,128)} %get-tuple-element.133) | copy-start | bytes 3076
  74.8 7.0 %copy-start.59 = (f32[1,1,256]{2,1,0:T(1,128)S(1)}, f32[1,1,256]{2,1,0:T(1,128)}, u32[]{:S(2)}) copy-start(f32[1,1,256]{2,1,0:T(1,128)} %get-tuple-element.134) | copy-start | bytes 3076
  74.8 7.0 %copy-start.61 = (f32[1,1,256]{2,1,0:T(1,128)S(1)}, f32[1,1,256]{2,1,0:T(1,128)}, u32[]{:S(2)}) copy-start(f32[1,1,256]{2,1,0:T(1,128)} %get-tuple-element.135) | copy-start | bytes 3076
  74.8 7.0 %copy-start.63 = (f32[1,1,256]{2,1,0:T(1,128)S(1)}, f32[1,1,256]{2,1,0:T(1,128)}, u32[]{:S(2)}) copy-start(f32[1,1,256]{2,1,0:T(1,128)} %get-tuple-element.136) | copy-start | bytes 3076
  74.8 7.0 %copy-start.65 = (f32[1,1,256]{2,1,0:T(1,128)S(1)}, f32[1,1,256]{2,1,0:T(1,128)}, u32[]{:S(2)}) copy-start(f32[1,1,256]{2,1,0:T(1,128)} %get-tuple-element.137) | copy-start | bytes 3076
  74.8 7.0 %copy-start.67 = (f32[1,1,256]{2,1,0:T(1,128)S(1)}, f32[1,1,256]{2,1,0:T(1,128)}, u32[]{:S(2)}) copy-start(f32[1,1,256]{2,1,0:T(1,128)} %copy-done.66) | copy-start | bytes 3076
  74.8 7.0 %copy-start.69 = (f32[1,1,256]{2,1,0:T(1,128)S(1)}, f32[1,1,256]{2,1,0:T(1,128)}, u32[]{:S(2)}) copy-start(f32[1,1,256]{2,1,0:T(1,128)} %copy-done.68) | copy-start | bytes 3076
  74.8 7.0 %copy-start.71 = (f32[1,1,256]{2,1,0:T(1,128)S(1)}, f32[1,1,256]{2,1,0:T(1,128)}, u32[]{:S(2)}) copy-start(f32[1,1,256]{2,1,0:T(1,128)} %copy-done.70) | copy-start | bytes 3076
  74.8 7.0 %copy-start.73 = (f32[1,1,256]{2,1,0:T(1,128)S(1)}, f32[1,1,256]{2,1,0:T(1,128)}, u32[]{:S(2)}) copy-start(f32[1,1,256]{2,1,0:T(1,128)} %copy-done.72) | copy-start | bytes 3076
  74.9 7.0 %copy-start.75 = (f32[1,1,256]{2,1,0:T(1,128)S(1)}, f32[1,1,256]{2,1,0:T(1,128)}, u32[]{:S(2)}) copy-start(f32[1,1,256]{2,1,0:T(1,128)} %copy-done.74) | copy-start | bytes 3076
  74.9 7.0 %copy-start.77 = (f32[1,1,256]{2,1,0:T(1,128)S(1)}, f32[1,1,256]{2,1,0:T(1,128)}, u32[]{:S(2)}) copy-start(f32[1,1,256]{2,1,0:T(1,128)} %copy-done.76) | copy-start | bytes 3076
  74.9 7.0 %copy-start.79 = (f32[1,1,256]{2,1,0:T(1,128)S(1)}, f32[1,1,256]{2,1,0:T(1,128)}, u32[]{:S(2)}) copy-start(f32[1,1,256]{2,1,0:T(1,128)} %copy-done.78) | copy-start | bytes 3076
  81.6 23.2 %copy-start.3 = (f32[64,32,256]{2,1,0:T(8,128)}, f32[64,32,256]{2,1,0:T(8,128)S(1)}, u32[]{:S(2)}) copy-start(f32[64,32,256]{2,1,0:T(8,128)S(1)} %get-tuple-element.89) | copy-start | bytes 6291460
  82.0 28.1 %copy-start.10 = (f32[256,1024]{1,0:T(8,128)S(1)}, f32[256,1024]{1,0:T(8,128)}, u32[]{:S(2)}) copy-start(f32[256,1024]{1,0:T(8,128)} %fusion.7) | copy-start | bytes 3145732
  82.0 28.0 %copy-start.11 = (f32[256,1024]{1,0:T(8,128)S(1)}, f32[256,1024]{1,0:T(8,128)}, u32[]{:S(2)}) copy-start(f32[256,1024]{1,0:T(8,128)} %fusion.122) | copy-start | bytes 3145732
  105.6 9.6 %collective-permute-start.6 = (bf16[70,3,256]{2,1,0:T(4,128)(2,1)S(1)}, bf16[70,3,256]{2,1,0:T(4,128)(2,1)}, u32[]{:S(2)}, u32[]{:S(2)}) collective-permute-start(bf16[70,3,256]{2,1,0:T(4,128)(2,1)S(1)} %get-tuple-element.94), channel_id=1, source_target_pairs={{0,1},{1,2},{2,3},{3,4},{4,5},{5,6},{6,7},{7,8},{8,9},{9,10},{10,1... | collective-permute-start | bytes 322568 | tf_op jit(solution)/shard_map/ppermute | solution.py:25
  106.2 9.0 %collective-permute-start.7 = (bf16[70,3,256]{2,1,0:T(4,128)(2,1)}, bf16[70,3,256]{2,1,0:T(4,128)(2,1)}, u32[]{:S(2)}, u32[]{:S(2)}) collective-permute-start(bf16[70,3,256]{2,1,0:T(4,128)(2,1)} %get-tuple-element.95), channel_id=1, source_target_pairs={{1,0},{2,1},{3,2},{4,3},{5,4},{6,5},{7,6},{8,7},{9,8},{10,9},{11,1... | collective-permute-start | bytes 322568 | tf_op jit(solution)/shard_map/ppermute | solution.py:27
  130.4 6.4 %collective-permute-start.8 = (bf16[3,32,256]{2,1,0:T(8,128)(2,1)S(1)}, bf16[3,32,256]{2,1,0:T(8,128)(2,1)}, u32[]{:S(2)}, u32[]{:S(2)}) collective-permute-start(bf16[3,32,256]{2,1,0:T(8,128)(2,1)S(1)} %slice.1409), channel_id=1, source_target_pairs={{0,1},{1,0},{2,3},{3,2},{4,5},{5,4},{6,7},{7,6},{8,9},{9,8},{10,11... | collective-permute-start | bytes 147464 | tf_op jit(solution)/shard_map/ppermute | solution.py:15
  136.8 6.3 %collective-permute-start.9 = (bf16[3,32,256]{2,1,0:T(8,128)(2,1)}, bf16[3,32,256]{2,1,0:T(8,128)(2,1)}, u32[]{:S(2)}, u32[]{:S(2)}) collective-permute-start(bf16[3,32,256]{2,1,0:T(8,128)(2,1)} %collective-permute-done.8), channel_id=1, source_target_pairs={{0,2},{2,0},{1,3},{3,1},{4,6},{6,4},{5,7},{7,5},{8,10},{10,8},{9,1... | collective-permute-start | bytes 147464 | tf_op jit(solution)/shard_map/ppermute | solution.py:15
  141.2 34.3 %copy-start.5 = (f32[70,32,256]{2,1,0:T(8,128)S(1)}, f32[70,32,256]{2,1,0:T(8,128)}, u32[]{:S(2)}) copy-start(f32[70,32,256]{2,1,0:T(8,128)} %scatter-add.11) | copy-start | bytes 6881284
  143.1 6.2 %collective-permute-start.10 = (bf16[3,32,256]{2,1,0:T(8,128)(2,1)}, bf16[3,32,256]{2,1,0:T(8,128)(2,1)S(1)}, u32[]{:S(2)}, u32[]{:S(2)}) collective-permute-start(bf16[3,32,256]{2,1,0:T(8,128)(2,1)} %collective-permute-done.9), channel_id=1, source_target_pairs={{0,4},{4,0},{1,5},{5,1},{2,6},{6,2},{3,7},{7,3},{8,12},{12,8},{9,1... | collective-permute-start | bytes 147464 | tf_op jit(solution)/shard_map/ppermute | solution.py:15
  149.2 27.8 %collective-permute-start.11 = (bf16[3,32,256]{2,1,0:T(8,128)(2,1)S(1)}, bf16[3,32,256]{2,1,0:T(8,128)(2,1)S(1)}, u32[]{:S(2)}, u32[]{:S(2)}) collective-permute-start(bf16[3,32,256]{2,1,0:T(8,128)(2,1)S(1)} %collective-permute-done.10), channel_id=1, source_target_pairs={{0,8},{8,0},{1,9},{9,1},{2,10},{10,2},{3,11},{11,3},{4,12},{12,4},... | collective-permute-start | bytes 147464 | tf_op jit(solution)/shard_map/ppermute | solution.py:15
  (57 other events, 281.4 us)
Sparse Core Ops, SparseCore 0:
  111.7 60.6 reduce-scatter.1
